TPU v7x, 32 devices: a whole 2x2x4 slice. The times are simulated.
32 devices in a mesh: wide: 8 (over z, y), narrow: 4 (over x, core).
Axes of the slice: x: 2, y: 2, z: 4, core: 2. Of those that a mesh axis runs over, the one named last changes fastest.
Arguments:
- media_feats: bfloat16 [8, 2048, 1536], P('wide', 'narrow'), may hold values from -6 to 6
- latents: bfloat16 [8, 64, 1536], P('wide', 'narrow'), may hold values from -6 to 6
- frame_counts: int32 [8], P('wide'), may hold values from 1 to 8, as said below
- media_mask: int32 [8, 2048], P('wide'), may hold values 0 or 1
- time_embed: bfloat16 [8, 1536], replicated, may hold values from -3 to 3
- media_gain: float32 [1536], replicated, may hold values from 0.1 to 1.9
- media_bias: float32 [1536], replicated, may hold values from -1.75 to 1.75
- latent_gain: float32 [1536], replicated, may hold values from 0.1 to 1.9
- latent_bias: float32 [1536], replicated, may hold values from -1.75 to 1.75
- ffn_gain: float32 [1536], replicated, may hold values from 0.1 to 1.9
- ffn_bias: float32 [1536], replicated, may hold values from -1.75 to 1.75
- query_weight: bfloat16 [1536, 1536], P('wide', 'narrow'), may hold values from -0.3125 to 0.3125
- keyval_weight: bfloat16 [1536, 2, 1536], P('wide', None, 'narrow'), may hold values from -0.15625 to 0.15625
- output_weight: bfloat16 [1536, 1536], P('narrow', 'wide'), may hold values from -0.625 to 0.625
- up_weight: bfloat16 [1536, 6144], P(None, 'narrow'), may hold values from -0.15625 to 0.15625
- down_weight: bfloat16 [6144, 1536], P('narrow'), may hold values from -0.078125 to 0.078125
- cotangent: bfloat16 [8, 64, 1536], P('wide', 'narrow'), may hold values from -6 to 6
Outputs:
- out_latents: bfloat16 [8, 64, 1536], P('wide', 'narrow')
- grad_media: bfloat16 [8, 2048, 1536], P('wide', 'narrow')
- grad_latents: bfloat16 [8, 64, 1536], P('wide', 'narrow')
- grad_time_embed: float32 [8, 1536], P(None, ('wide', 'narrow'))
- grad_media_gain: float32 [1536], P(('wide', 'narrow'))
- grad_media_bias: float32 [1536], P(('wide', 'narrow'))
- grad_latent_gain: float32 [1536], P(('wide', 'narrow'))
- grad_latent_bias: float32 [1536], P(('wide', 'narrow'))
- grad_ffn_gain: float32 [1536], P(('wide', 'narrow'))
- grad_ffn_bias: float32 [1536], P(('wide', 'narrow'))
- grad_query_weight: float32 [1536, 1536], P('wide', 'narrow')
- grad_keyval_weight: float32 [1536, 2, 1536], P('wide', None, 'narrow')
- grad_output_weight: float32 [1536, 1536], P('narrow', 'wide')
- grad_up_weight: float32 [1536, 6144], P('wide', 'narrow')
- grad_down_weight: float32 [6144, 1536], P('narrow', 'wide')
Inputs may be any that keep to these rules, and one draw needn't show every extreme that they name: `frame_counts`: frames of each item; some item has exactly 8.
All inputs are finite; a program needn't handle non-finite values. No bound on the sum of `media_mask` on one device may be relied on, other than what follows from the above.
Results may differ from a plain program's by a relative error of at most 0.02.
Values may be sent and summed in bfloat16 or wider, within the bound.
A program may use at most 128 MiB of HBM per device.

v0:
```python
import math
import jax
import jax.numpy as jnp
from jax import lax
from jax.sharding import PartitionSpec as P

HEADS = 16
HEAD_DIM = 96
FRAMES_MAX = 8
PATCHES = 256
EPS = 1e-05
ENT_COEF = 4.0
HIGH = lax.Precision.HIGHEST


def norm_forward(values, norm_gain, norm_bias):
    row_mean = jnp.mean(values, axis=-1, keepdims=True)
    centered = values - row_mean
    inv_std = lax.rsqrt(jnp.mean(centered * centered, axis=-1, keepdims=True) + EPS)
    normed = centered * inv_std
    return (normed * norm_gain + norm_bias, normed, inv_std)


def norm_backward(grad_out, normed, inv_std, norm_gain):
    scaled = grad_out * norm_gain
    grad_in = inv_std * (
        scaled
        - jnp.mean(scaled, axis=-1, keepdims=True)
        - normed * jnp.mean(scaled * normed, axis=-1, keepdims=True)
    )
    return (grad_in, jnp.sum(grad_out * normed, axis=0), jnp.sum(grad_out, axis=0))


def gelu_slope(pre_act):
    cdf_part = 0.5 * (1.0 + lax.erf(pre_act * (1.0 / math.sqrt(2.0))))
    density = jnp.exp(-0.5 * pre_act * pre_act) * (1.0 / math.sqrt(2.0 * math.pi))
    return cdf_part + pre_act * density


def body(
    media_feats,
    latents,
    frame_counts,
    media_mask,
    time_embed,
    media_gain,
    media_bias,
    latent_gain,
    latent_bias,
    ffn_gain,
    ffn_bias,
    query_weight,
    keyval_weight,
    output_weight,
    up_weight,
    down_weight,
    cotangent,
):
    item_count = media_feats.shape[0]
    own_media = media_feats.shape[1]
    width = media_feats.shape[2]
    own_latent = latents.shape[1]
    narrow_size = lax.axis_size("narrow")
    narrow_pos = lax.axis_index("narrow")
    media_total = own_media * narrow_size
    latent_total = own_latent * narrow_size
    head_local = HEADS // narrow_size
    cols = head_local * HEAD_DIM
    key_total = media_total + latent_total
    all_ids = jnp.arange(media_total, dtype=jnp.int32) // PATCHES
    valid_tok = (all_ids[None, :] < frame_counts[:, None]) & (media_mask > 0)
    local_count = jnp.sum(valid_tok.astype(jnp.float32)) + float(item_count * latent_total)
    total_count = lax.psum(local_count, "wide")
    all_items = item_count * lax.axis_size("wide")
    ent_weight = ENT_COEF * float(all_items * media_total) / total_count
    query_own, keyval_own, output_own = (
        lax.all_gather(query_weight, "wide", axis=0, tiled=True),
        lax.all_gather(keyval_weight, "wide", axis=0, tiled=True),
        lax.all_gather(output_weight, "wide", axis=1, tiled=True),
    )
    query_full, keyval_full = (
        lax.all_gather(query_own, "narrow", axis=1, tiled=True),
        lax.all_gather(keyval_own, "narrow", axis=2, tiled=True),
    )
    keyval_flat = keyval_own.reshape(width, 2 * cols)
    own_ids = (narrow_pos * own_media + jnp.arange(own_media, dtype=jnp.int32)) // PATCHES
    frame_onehot = own_ids[:, None] == jnp.arange(FRAMES_MAX, dtype=jnp.int32)[None, :]
    time_rows = jnp.dot(
        frame_onehot.astype(jnp.bfloat16), time_embed, preferred_element_type=jnp.float32
    )
    score_scale = HEAD_DIM ** (-0.5)

    def item_step(carry, item):
        (
            down_acc,
            up_acc,
            output_acc,
            keyval_acc,
            query_acc,
            mg_acc,
            mb_acc,
            lg_acc,
            lb_acc,
            fg_acc,
            fb_acc,
            time_acc,
        ) = carry
        media_one, latent_one, valid_one, cot_one = item
        media_nf, media_hat, media_istd = norm_forward(
            media_one.astype(jnp.float32) + time_rows, media_gain, media_bias
        )
        latent_f32 = latent_one.astype(jnp.float32)
        latent_nf, latent_hat, latent_istd = norm_forward(latent_f32, latent_gain, latent_bias)
        media_all, latent_all = (
            lax.all_gather(media_nf.astype(jnp.bfloat16), "narrow", axis=0, tiled=True),
            lax.all_gather(latent_nf.astype(jnp.bfloat16), "narrow", axis=0, tiled=True),
        )
        keys_in = jnp.concatenate([media_all, latent_all], axis=0)
        query_act = jnp.dot(latent_all, query_own, preferred_element_type=jnp.float32).astype(
            jnp.bfloat16
        )
        key_vals = jnp.dot(keys_in, keyval_flat, preferred_element_type=jnp.float32).astype(
            jnp.bfloat16
        )
        query_heads = query_act.reshape(latent_total, head_local, HEAD_DIM)
        key_heads = key_vals[:, :cols].reshape(key_total, head_local, HEAD_DIM)
        value_heads = key_vals[:, cols:].reshape(key_total, head_local, HEAD_DIM)
        key_valid = jnp.concatenate([valid_one, jnp.ones((latent_total,), dtype=bool)])
        scores = (
            jnp.einsum("lhd,khd->hlk", query_heads, key_heads, preferred_element_type=jnp.float32)
            * score_scale
        )
        open_keys = key_valid[None, None, :]
        masked = jnp.where(open_keys, scores, -1e30)
        row_top = jnp.max(masked, axis=-1)
        expo = jnp.exp(masked - row_top[..., None])
        prob_all = expo / jnp.sum(expo, axis=-1)[..., None]
        prob_low = prob_all.astype(jnp.bfloat16)
        plain_scores = jnp.where(open_keys, scores, 0.0)
        mean_score = jnp.sum(prob_all * plain_scores, axis=-1)
        attn_out = jnp.einsum(
            "hlk,khd->lhd", prob_low, value_heads, preferred_element_type=jnp.float32
        ).reshape(latent_total, cols)
        attn_low = attn_out.astype(jnp.bfloat16)
        branch_part = jnp.dot(attn_low, output_own, preferred_element_type=jnp.float32)
        branch_own = lax.psum_scatter(
            branch_part.astype(jnp.bfloat16), "narrow", scatter_dimension=0, tiled=True
        ).astype(jnp.float32)
        latent_mid = latent_f32 + branch_own
        hidden_f, hidden_hat, hidden_istd = norm_forward(latent_mid, ffn_gain, ffn_bias)
        hidden_all, cot_all = (
            lax.all_gather(hidden_f.astype(jnp.bfloat16), "narrow", axis=0, tiled=True),
            lax.all_gather(cot_one, "narrow", axis=0, tiled=True),
        )
        pre_act = jnp.dot(hidden_all, up_weight, preferred_element_type=jnp.float32)
        act_low = jax.nn.gelu(pre_act, approximate=False).astype(jnp.bfloat16)
        ffn_part = jnp.dot(act_low, down_weight, preferred_element_type=jnp.float32)
        ffn_own = lax.psum_scatter(
            ffn_part.astype(jnp.bfloat16), "narrow", scatter_dimension=0, tiled=True
        ).astype(jnp.float32)
        out_one = (latent_mid + ffn_own).astype(jnp.bfloat16)
        down_acc = down_acc + jnp.einsum(
            "lf,ld->fd", act_low, cot_all, preferred_element_type=jnp.float32
        )
        grad_act = jnp.einsum("ld,fd->lf", cot_all, down_weight, preferred_element_type=jnp.float32)
        grad_pre = (grad_act * gelu_slope(pre_act)).astype(jnp.bfloat16)
        up_acc = up_acc + jnp.einsum(
            "ld,lf->df", hidden_all, grad_pre, preferred_element_type=jnp.float32
        )
        hidden_part = jnp.einsum(
            "lf,df->ld", grad_pre, up_weight, preferred_element_type=jnp.float32
        )
        grad_hidden = lax.psum_scatter(
            hidden_part.astype(jnp.bfloat16), "narrow", scatter_dimension=0, tiled=True
        ).astype(jnp.float32)
        grad_norm, fg_part, fb_part = norm_backward(grad_hidden, hidden_hat, hidden_istd, ffn_gain)
        grad_mid = cot_one.astype(jnp.float32) + grad_norm
        grad_branch_all = lax.all_gather(
            grad_mid.astype(jnp.bfloat16), "narrow", axis=0, tiled=True
        )
        output_acc = output_acc + jnp.einsum(
            "lc,ld->cd", attn_low, grad_branch_all, preferred_element_type=jnp.float32
        )
        grad_attn = jnp.einsum(
            "ld,cd->lc", grad_branch_all, output_own, preferred_element_type=jnp.float32
        ).astype(jnp.bfloat16)
        row_dots = jnp.sum(
            (grad_attn.astype(jnp.float32) * attn_out).reshape(latent_total, head_local, HEAD_DIM),
            axis=-1,
        )
        shift_rows = (jnp.transpose(row_dots, (1, 0)) - ent_weight * mean_score)[..., None]
        grad_heads = grad_attn.reshape(latent_total, head_local, HEAD_DIM)
        grad_prob = jnp.einsum(
            "lhd,khd->hlk", grad_heads, value_heads, preferred_element_type=jnp.float32
        )
        grad_scores = (prob_all * (grad_prob - ent_weight * plain_scores - shift_rows)).astype(
            jnp.bfloat16
        )
        grad_values = jnp.einsum(
            "hlk,lhd->khd", prob_low, grad_heads, preferred_element_type=jnp.float32
        ).reshape(key_total, cols)
        grad_keys = (
            jnp.einsum(
                "hlk,lhd->khd", grad_scores, query_heads, preferred_element_type=jnp.float32
            ).reshape(key_total, cols)
            * score_scale
        )
        grad_query = (
            jnp.einsum(
                "hlk,khd->lhd", grad_scores, key_heads, preferred_element_type=jnp.float32
            ).reshape(latent_total, cols)
            * score_scale
        ).astype(jnp.bfloat16)
        grad_pairs = jnp.concatenate([grad_keys, grad_values], axis=-1).astype(jnp.bfloat16)
        keyval_acc = keyval_acc + jnp.einsum(
            "kd,ke->de", keys_in, grad_pairs, preferred_element_type=jnp.float32
        )
        query_acc = query_acc + jnp.einsum(
            "ld,lc->dc", latent_all, grad_query, preferred_element_type=jnp.float32
        )
        media_pairs = grad_pairs[:media_total].reshape(media_total, 2, cols)
        latent_pairs = jnp.concatenate(
            [
                grad_pairs[media_total:].reshape(latent_total, 2, cols),
                grad_query.reshape(latent_total, 1, cols),
            ],
            axis=1,
        )
        media_back, latent_back = (
            lax.all_to_all(media_pairs, "narrow", split_axis=0, concat_axis=2, tiled=True),
            lax.all_to_all(latent_pairs, "narrow", split_axis=0, concat_axis=2, tiled=True),
        )
        grad_media_rows = jnp.einsum(
            "rsc,dsc->rd", media_back, keyval_full, preferred_element_type=jnp.float32
        )
        grad_latent_normed = jnp.einsum(
            "rsc,dsc->rd", latent_back[:, :2], keyval_full, preferred_element_type=jnp.float32
        ) + jnp.einsum(
            "rc,dc->rd", latent_back[:, 2], query_full, preferred_element_type=jnp.float32
        )
        grad_media_in, mg_part, mb_part = norm_backward(
            grad_media_rows, media_hat, media_istd, media_gain
        )
        time_acc = time_acc + jnp.einsum(
            "mf,md->fd", frame_onehot.astype(jnp.float32), grad_media_in, precision=HIGH
        )
        grad_latent_in, lg_part, lb_part = norm_backward(
            grad_latent_normed, latent_hat, latent_istd, latent_gain
        )
        grad_latent_one = (grad_mid + grad_latent_in).astype(jnp.bfloat16)
        carry = (
            down_acc,
            up_acc,
            output_acc,
            keyval_acc,
            query_acc,
            mg_acc + mg_part,
            mb_acc + mb_part,
            lg_acc + lg_part,
            lb_acc + lb_part,
            fg_acc + fg_part,
            fb_acc + fb_part,
            time_acc,
        )
        return (carry, (out_one, grad_media_in.astype(jnp.bfloat16), grad_latent_one))

    ff_local = up_weight.shape[1]
    vector_zero = jnp.zeros((width,), jnp.float32)
    start = (
        jnp.zeros((ff_local, width), jnp.float32),
        jnp.zeros((width, ff_local), jnp.float32),
        jnp.zeros((cols, width), jnp.float32),
        jnp.zeros((width, 2 * cols), jnp.float32),
        jnp.zeros((width, cols), jnp.float32),
        vector_zero,
        vector_zero,
        vector_zero,
        vector_zero,
        vector_zero,
        vector_zero,
        jnp.zeros((FRAMES_MAX, width), jnp.float32),
    )
    totals, stacked = lax.scan(item_step, start, (media_feats, latents, valid_tok, cotangent))
    (
        down_acc,
        up_acc,
        output_acc,
        keyval_acc,
        query_acc,
        mg_acc,
        mb_acc,
        lg_acc,
        lb_acc,
        fg_acc,
        fb_acc,
        time_acc,
    ) = totals
    out_latents, grad_media, grad_latents = stacked
    up_sum, down_sum, query_sum, keyval_sum, output_sum = (
        lax.psum_scatter(
            up_acc.astype(jnp.bfloat16), "wide", scatter_dimension=0, tiled=True
        ).astype(jnp.float32),
        lax.psum_scatter(
            down_acc.astype(jnp.bfloat16), "wide", scatter_dimension=1, tiled=True
        ).astype(jnp.float32),
        lax.psum_scatter(
            query_acc.astype(jnp.bfloat16), "wide", scatter_dimension=0, tiled=True
        ).astype(jnp.float32),
        lax.psum_scatter(
            keyval_acc.reshape(width, 2, cols).astype(jnp.bfloat16),
            "wide",
            scatter_dimension=0,
            tiled=True,
        ).astype(jnp.float32),
        lax.psum_scatter(
            output_acc.astype(jnp.bfloat16), "wide", scatter_dimension=1, tiled=True
        ).astype(jnp.float32),
    )
    mg_sum, mb_sum, lg_sum, lb_sum, fg_sum, fb_sum, time_sum = (
        lax.psum_scatter(mg_acc, ("wide", "narrow"), scatter_dimension=0, tiled=True),
        lax.psum_scatter(mb_acc, ("wide", "narrow"), scatter_dimension=0, tiled=True),
        lax.psum_scatter(lg_acc, ("wide", "narrow"), scatter_dimension=0, tiled=True),
        lax.psum_scatter(lb_acc, ("wide", "narrow"), scatter_dimension=0, tiled=True),
        lax.psum_scatter(fg_acc, ("wide", "narrow"), scatter_dimension=0, tiled=True),
        lax.psum_scatter(fb_acc, ("wide", "narrow"), scatter_dimension=0, tiled=True),
        lax.psum_scatter(time_acc, ("wide", "narrow"), scatter_dimension=1, tiled=True),
    )
    return (
        out_latents,
        grad_media,
        grad_latents,
        time_sum,
        mg_sum,
        mb_sum,
        lg_sum,
        lb_sum,
        fg_sum,
        fb_sum,
        query_sum,
        keyval_sum,
        output_sum,
        up_sum,
        down_sum,
    )


def solution(mesh):
    placed = (
        P("wide", "narrow", None),
        P("wide", "narrow", None),
        P("wide"),
        P("wide", None),
        P(),
        P(),
        P(),
        P(),
        P(),
        P(),
        P(),
        P("wide", "narrow"),
        P("wide", None, "narrow"),
        P("narrow", "wide"),
        P(None, "narrow"),
        P("narrow", None),
        P("wide", "narrow", None),
    )
    return jax.shard_map(
        body,
        mesh=mesh,
        in_specs=placed,
        out_specs=(
            P("wide", "narrow", None),
            P("wide", "narrow", None),
            P("wide", "narrow", None),
            P(None, ("wide", "narrow")),
            P(("wide", "narrow")),
            P(("wide", "narrow")),
            P(("wide", "narrow")),
            P(("wide", "narrow")),
            P(("wide", "narrow")),
            P(("wide", "narrow")),
            P("wide", "narrow"),
            P("wide", None, "narrow"),
            P("narrow", "wide"),
            P("wide", "narrow"),
            P("narrow", "wide"),
        ),
        check_vma=False,
    )
```

profile of v0, /device:TPU:0, one launch (start us, length us, event | category | flops | bytes accessed | tf_op | source)
XLA Modules:
  0.0 941.4 jit_solution(12498868731809088327)
XLA Ops:
  15.3 6.9 all_gather.36
  23.6 30.5 %all-gather.12.cloned.1.call-done = bf16[1536,384]{1,0:T(8,128)(2,1)} async-done(((bf16[192,384]{1,0:T(8,128)(2,1)}), bf16[1536,384]{1,0:T(8,128)(2,1)}) %all-gather.12.cloned.1.call-update) | async-done | bytes 1179664 | tf_op jit(solution)/shard_map/all_gather | solution.py:77
  55.8 51.6 %all-gather.10.cloned.1.call-done = bf16[1536,2,384]{2,0,1:T(8,128)(2,1)} async-done(((bf16[192,2,384]{2,0,1:T(8,128)(2,1)}), bf16[1536,2,384]{2,0,1:T(8,128)(2,1)}) %all-gather.10.cloned.1.call-update) | async-done | bytes 2359312 | tf_op jit(solution)/shard_map/all_gather | solution.py:78
  111.7 42.8 %all-gather.8.cloned.1.call-done = bf16[2048,1536]{1,0:T(8,128)(2,1)} async-done(((bf16[512,1536]{1,0:T(8,128)(2,1)}), bf16[2048,1536]{1,0:T(8,128)(2,1)}) %all-gather.8.cloned.1.call-update) | async-done | bytes 6291472 | tf_op jit(solution)/shard_map/while/body/eval_jaxpr/all_gather | solution.py:115
  181.3 16.3 %all-gather.14.cloned.1.call-done = bf16[384,1536]{0,1:T(8,128)(2,1)} async-done(((bf16[384,192]{0,1:T(8,128)(2,1)}), bf16[384,1536]{0,1:T(8,128)(2,1)}) %all-gather.14.cloned.1.call-update) | async-done | bytes 1179664 | tf_op jit(solution)/shard_map/all_gather | solution.py:79
  200.1 7.1 all-gather
  207.2 11.8 %reduce-scatter.11.cloned.1.call-done = bf16[16,1536]{1,0:T(8,128)(2,1)} async-done(((bf16[64,1536]{1,0:T(8,128)(2,1)}), bf16[16,1536]{1,0:T(8,128)(2,1)}) %reduce-scatter.11.cloned.1.call-update) | async-done | bytes 49168 | tf_op jit(solution)/shard_map/while/body/eval_jaxpr/reduce_scatter | solution.py:146
  221.9 5.6 all_gather.40
  241.6 19.1 %reduce-scatter.15.cloned.1.call-done = bf16[16,1536]{1,0:T(8,128)(2,1)} async-done(((bf16[64,1536]{1,0:T(8,128)(2,1)}), bf16[16,1536]{1,0:T(8,128)(2,1)}) %reduce-scatter.15.cloned.1.call-update) | async-done | bytes 49168 | tf_op jit(solution)/shard_map/while/body/eval_jaxpr/reduce_scatter | solution.py:173
  263.2 5.6 all_gather.42
  272.6 22.0 %psum.7 = f32[]{:T(128)} all-reduce(f32[]{:T(128)S(6)} %add.196), channel_id=1, replica_groups=mesh['wide'=8,'narrow'=4] {'wide'}, use_global_device_ids=true, to_apply=%region_14.15 | all-reduce | flops 1 | bytes 8 | tf_op jit(solution)/shard_map/psum | solution.py:73
  316.8 10.9 %convolution_convert_fusion.4 = bf16[1536,768]{0,1:T(8,128)(2,1)} fusion(bf16[2112,1536]{1,0:T(8,128)(2,1)} %copy-done.6, bf16[2112,384]{0,1:T(8,128)(2,1)S(1)} %bitcast.160, bf16[2112,384]{0,1:T(8,128)(2,1)S(1)} %bitcast.155), kind=kOutput, calls=%fused_computation.19 | convolution fusion | flops 4990500864 | bytes 12091392 | tf_op jit(solution)/shard_map/while/body/eval_jaxpr/kd,ke->de/dot_general | solution.py:215
  327.7 6.9 copy.135
  338.8 8.7 copy.126
  357.3 31.9 %all-to-all-done = bf16[2048,2,384]{2,1,0:T(2,128)(2,1)} async-done(((bf16[2048,2,384]{2,1,0:T(2,128)(2,1)}), bf16[2048,2,384]{2,1,0:T(2,128)(2,1)}, u32[]{:S(2)}, u32[]{:S(2)}) %all-to-all-start) | async-done | bytes 3145760 | tf_op jit(solution)/shard_map/while/body/eval_jaxpr/all_to_all | solution.py:230
  393.5 10.0 %multiply_reduce_fusion = (f32[1536]{0:T(1024)}, f32[512]{0:T(512)S(1)}, f32[512]{0:T(512)S(1)}, f32[1536]{0:T(1024)}, f32[512,1536]{1,0:T(8,128)S(1)}) fusion(f32[512,1536]{1,0:T(8,128)S(1)} %get-tuple-element.150, f32[512]{0:T(512)S(1)} %add_rsqrt_fusion, f32[512]{0:T(512)S(1)} %broadcast_multiply_fusion.2, f32[1536]{0:T(1024)S(1)} %copy-done.33, ...), kind=kOutput, calls=%fused_computation.23 | convolution fusion | flops 4838912000 | bytes 18900992 | tf_op jit(solution)/shard_map/while/body/eval_jaxpr/rsc,dsc->rd/dot_general | solution.py:233
  431.6 31.3 %reduce-scatter.17.cloned.1.call-done = bf16[192,384]{1,0:T(8,128)(2,1)} async-done(((bf16[1536,384]{1,0:T(8,128)(2,1)}), bf16[192,384]{1,0:T(8,128)(2,1)}) %reduce-scatter.17.cloned.1.call-update) | async-done | bytes 147472 | tf_op jit(solution)/shard_map/reduce_scatter | solution.py:306
  464.6 109.4 %all-reduce.11.cloned.1.call-done = bf16[1536,2,384]{2,1,0:T(2,128)(2,1)} async-done(((bf16[1536,2,384]{2,1,0:T(2,128)(2,1)}), bf16[1536,2,384]{2,1,0:T(2,128)(2,1)}) %all-reduce.11.cloned.1.call-update) | async-done | bytes 2359312
  576.0 6.2 convolution_bitcast_fusion.2
  582.3 29.8 %all-gather.18.cloned.1.call-done = bf16[1536,1536]{1,0:T(8,128)(2,1)} async-done(((bf16[1536,384]{1,0:T(8,128)(2,1)}), bf16[1536,1536]{1,0:T(8,128)(2,1)}) %all-gather.18.cloned.1.call-update) | async-done | bytes 4718608 | tf_op jit(solution)/shard_map/all_gather | solution.py:82
  616.0 40.1 %all-reduce.8 = (f32[1536]{0:T(1024)S(1)}, f32[1536]{0:T(1024)S(1)}, f32[1536]{0:T(1024)S(1)}, f32[1536]{0:T(1024)S(1)}, f32[1536]{0:T(1024)S(1)}, /*index=5*/f32[1536]{0:T(1024)S(1)}) all-reduce(f32[1536]{0:T(1024)S(1)} %copy-done.46, f32[1536]{0:T(1024)S(1)} %copy-done.47, ...), channel_id=7, replica_groups=mesh['wide'=8,'narrow'=4] {'wide','narrow'}, use_global_device_ids=true, to_apply=%region_23.24.clone | all-reduce | flops 9216 | bytes 73728
  661.2 74.4 %reduce-scatter.25.cloned.1.call-done = f32[48,8]{1,0:T(8,128)} async-done(((f32[1536,8]{1,0:T(8,128)}), f32[48,8]{1,0:T(8,128)}) %reduce-scatter.25.cloned.1.call-update) | async-done | bytes 1552
  737.0 96.9 %reduce-scatter.21.cloned.1.call-done = bf16[192,1536]{1,0:T(8,128)(2,1)} async-done(((bf16[1536,1536]{1,0:T(8,128)(2,1)}), bf16[192,1536]{1,0:T(8,128)(2,1)}) %reduce-scatter.21.cloned.1.call-update) | async-done | bytes 589840 | tf_op jit(solution)/shard_map/reduce_scatter | solution.py:300
  836.0 96.6 %reduce-scatter.23.cloned.1.call-done = bf16[1536,192]{0,1:T(8,128)(2,1)} async-done(((bf16[1536,1536]{0,1:T(8,128)(2,1)}), bf16[1536,192]{0,1:T(8,128)(2,1)}) %reduce-scatter.23.cloned.1.call-update) | async-done | bytes 589840 | tf_op jit(solution)/shard_map/reduce_scatter | solution.py:303
  (242 shorter events, 151.6 us)
Async XLA Ops:
  7.2 46.9 %all-gather.12.cloned.1.call-start = ((), (), s32[]{:S(2)}) async-start(), calls=%async_computation.12 | async-start | bytes 1327104 | tf_op jit(solution)/shard_map/all_gather | solution.py:77
  7.9 99.4 %all-gather.10.cloned.1.call-start = ((), (), s32[]{:S(2)}) async-start(), calls=%async_computation.11 | async-start | bytes 2654208 | tf_op jit(solution)/shard_map/all_gather | solution.py:78
  9.7 144.7 %all-gather.8.cloned.1.call-start = ((), (), s32[]{:S(2)}) async-start(), calls=%async_computation.10 | async-start | bytes 7864320 | tf_op jit(solution)/shard_map/while/body/eval_jaxpr/all_gather | solution.py:115
  14.2 183.4 %all-gather.14.cloned.1.call-start = ((), (), s32[]{:S(2)}) async-start(), calls=%async_computation.13 | async-start | bytes 1327104 | tf_op jit(solution)/shard_map/all_gather | solution.py:79
  14.8 204.2 %reduce-scatter.11.cloned.1.call-start = ((), (), s32[]{:S(2)}) async-start(), calls=%async_computation.14 | async-start | bytes 245760 | tf_op jit(solution)/shard_map/while/body/eval_jaxpr/reduce_scatter | solution.py:146
  23.5 149.4 %copy-start.54 = (pred[2112]{0:T(1024)(128)(4,1)}, pred[2112]{0:T(1024)(128)(4,1)S(1)}, u32[]{:S(2)}) copy-start(pred[2112]{0:T(1024)(128)(4,1)S(1)} %concatenate.18) | copy-start | bytes 6340
  55.8 117.2 %copy-start.27 = (bf16[64,4,96]{2,1,0:T(4,128)(2,1)}, bf16[64,4,96]{2,1,0:T(4,128)(2,1)S(1)}, u32[]{:S(2)}) copy-start(bf16[64,4,96]{2,1,0:T(4,128)(2,1)S(1)} %reshape.235) | copy-start | bytes 147460
  176.6 127.5 %copy-start.57 = (f32[4,64]{1,0:T(4,128)}, f32[4,64]{1,0:T(4,128)S(1)}, u32[]{:S(2)}) copy-start(f32[4,64]{1,0:T(4,128)S(1)} %get-tuple-element.151) | copy-start | bytes 3076
  200.1 60.6 %reduce-scatter.15.cloned.1.call-start = ((), (), s32[]{:S(2)}) async-start(), calls=%async_computation.16 | async-start | bytes 245760 | tf_op jit(solution)/shard_map/while/body/eval_jaxpr/reduce_scatter | solution.py:173
  240.8 152.7 %all-gather.16.cloned.1.call-start = ((), (), s32[]{:S(2)}) async-start(), calls=%async_computation.17 | async-start | bytes 11796480 | tf_op jit(solution)/shard_map/all_gather | solution.py:83
  241.5 188.5 %reduce-scatter.19.cloned.1.call-start = ((), (), s32[]{:S(2)}) async-start(), calls=%async_computation.20 | async-start | bytes 1327104 | tf_op jit(solution)/shard_map/reduce_scatter | solution.py:315
  271.9 191.0 %reduce-scatter.17.cloned.1.call-start = ((), (), s32[]{:S(2)}) async-start(), calls=%async_computation.19 | async-start | bytes 1327104 | tf_op jit(solution)/shard_map/reduce_scatter | solution.py:306
  311.9 262.1 %all-reduce.11.cloned.1.call-start = ((), (), s32[]{:S(2)}) async-start(), calls=%async_computation.24 | async-start | bytes 4718592
  334.6 277.5 %all-gather.18.cloned.1.call-start = ((), (), s32[]{:S(2)}) async-start(), calls=%async_computation.18 | async-start | bytes 5898240 | tf_op jit(solution)/shard_map/all_gather | solution.py:82
  347.6 41.7 %all-to-all-start = ((bf16[2048,2,384]{2,1,0:T(2,128)(2,1)}), bf16[2048,2,384]{2,1,0:T(2,128)(2,1)}, u32[]{:S(2)}, u32[]{:S(2)}) async-start(bf16[2048,2,384]{2,1,0:T(2,128)(2,1)} %copy.126), calls=%async_computation.3 | async-start | bytes 6291456 | tf_op jit(solution)/shard_map/while/body/eval_jaxpr/all_to_all | solution.py:230
  352.3 307.3 %reduce-scatter.13.cloned.1.call-start = ((), (), s32[]{:S(2)}) async-start(), calls=%async_computation.15 | async-start | bytes 245760 | tf_op jit(solution)/shard_map/while/body/eval_jaxpr/reduce_scatter | solution.py:158
  357.0 378.5 %reduce-scatter.25.cloned.1.call-start = ((), (), s32[]{:S(2)}) async-start(), calls=%async_computation.23 | async-start | bytes 811008
  409.3 424.6 %reduce-scatter.21.cloned.1.call-start = ((), (), s32[]{:S(2)}) async-start(), calls=%async_computation.21 | async-start | bytes 5308416 | tf_op jit(solution)/shard_map/reduce_scatter | solution.py:300
  412.9 519.8 %reduce-scatter.23.cloned.1.call-start = ((), (), s32[]{:S(2)}) async-start(), calls=%async_computation.22 | async-start | bytes 5308416 | tf_op jit(solution)/shard_map/reduce_scatter | solution.py:303
  421.3 8.6 all-to-all-start.1
  582.2 77.3 %copy-start.24 = (bf16[16,1536]{1,0:T(8,128)(2,1)S(1)}, bf16[16,1536]{1,0:T(8,128)(2,1)}, u32[]{:S(2)}) copy-start(bf16[16,1536]{1,0:T(8,128)(2,1)} %reduce-scatter.15.cloned.1.call-done) | copy-start | bytes 147460
  582.2 77.3 %copy-start.26 = (bf16[1,16,1536]{2,1,0:T(8,128)(2,1)S(1)}, bf16[1,16,1536]{2,1,0:T(8,128)(2,1)}, u32[]{:S(2)}) copy-start(bf16[1,16,1536]{2,1,0:T(8,128)(2,1)} %param.33) | copy-start | bytes 147460
  582.3 77.3 %copy-start.37 = (f32[16]{0:T(128)S(1)}, f32[16]{0:T(128)}, u32[]{:S(2)}) copy-start(f32[16]{0:T(128)} %copy-done.36) | copy-start | bytes 196
  612.1 322.7 %copy-start.1 = (bf16[8,1536]{1,0:T(8,128)(2,1)S(1)}, bf16[8,1536]{1,0:T(8,128)(2,1)}, u32[]{:S(2)}) copy-start(bf16[8,1536]{1,0:T(8,128)(2,1)} %param.21) | copy-start | bytes 73732
  (52 other events, 939.6 us)
Sparse Core Ops, SparseCore 0:
  10.2 43.8 all-gather.11
  56.8 50.4 all-gather.9
  109.5 44.8 all-gather.7
  156.5 41.1 all-gather.13
  200.5 18.4 reduce-scatter.10
  240.9 19.7 reduce-scatter.14
  262.3 64.0 all-gather.15
  330.4 64.8 reduce-scatter.18
  399.2 63.7 reduce-scatter.16
  466.4 107.5 all-reduce.10
  575.6 36.5 all-gather.17
  614.4 19.8 reduce-scatter.12
  639.4 96.1 reduce-scatter.24
  739.1 94.7 reduce-scatter.20
  837.3 95.2 reduce-scatter.22
where the time goes:
time: 944 us; the launch traced here: 941 us
  waiting for transfers between devices  649 us (69%)
  matrix products  95.8 us (10%)
  blocking collectives  87.2 us (9%)
  local copies, waits for them, and re-layouts  54.7 us (6%)
  other arithmetic  28.2 us (3%)
  between operations  17.4 us (2%)
    unnamed x17, waiting for transfers between devices  187 us
    reduce_scatter x1, waiting for transfers between devices, body(): lax.psum_scatter(up_acc.astype(jnp.bfloat16), 'wide', scatter_dimension=0...  96.9 us
    reduce_scatter x1, waiting for transfers between devices, body(): lax.psum_scatter(down_acc.astype(jnp.bfloat16), 'wide', scatter_dimension...  96.6 us
    all_gather x1, waiting for transfers between devices, body(): lax.all_gather(keyval_weight, 'wide', axis=0, tiled=True)  51.6 us
    all_gather x1, waiting for transfers between devices, item_step(): lax.all_gather(media_nf.astype(jnp.bfloat16), 'narrow', axis=0, tiled=True)  42.8 us
    unnamed x1, blocking collectives  40.1 us
    all_to_all x1, waiting for transfers between devices, item_step(): lax.all_to_all(media_pairs, 'narrow', split_axis=0, concat_axis=2, tiled=...  31.9 us
    reduce_scatter x1, waiting for transfers between devices, body(): lax.psum_scatter(query_acc.astype(jnp.bfloat16), 'wide', scatter_dimensio...  31.3 us
  transfers between devices with their start and end apart: 17, of which 14 were waited for; matrix products, arithmetic and copies ran while one was open for 16% of the time, Pallas kernels for 0%

commit v1 on v0

--- a/solution.py
+++ b/solution.py
@@ -11,6 +11,28 @@
 EPS = 1e-05
 ENT_COEF = 4.0
 HIGH = lax.Precision.HIGHEST
+
+
+def laid_out(tiles, dim):
+    tiles = jnp.moveaxis(tiles, 0, dim)
+    dims = tiles.shape
+    return tiles.reshape(*dims[:dim], dims[dim] * dims[dim + 1], *dims[dim + 2 :])
+
+
+def ring_gather(x, axis, dim):
+    size = lax.axis_size(axis)
+    pairs = [(i, (i + 1) % size) for i in range(size)]
+    back = [(b, a) for a, b in pairs]
+    lower, upper = ([], [])
+    for step in range(size - 1):
+        if step % 2 == 0:
+            lower.append(lax.ppermute(lower[-1] if lower else x, axis, pairs))
+        else:
+            upper.append(lax.ppermute(upper[-1] if upper else x, axis, back))
+    parts = jnp.stack([*lower[::-1], x, *upper])
+    shift = lax.axis_index(axis) - len(lower)
+    parts = parts[(jnp.arange(size) - shift) % size]
+    return laid_out(parts, dim)
 
 
 def norm_forward(values, norm_gain, norm_bias):
@@ -74,7 +96,7 @@
     all_items = item_count * lax.axis_size("wide")
     ent_weight = ENT_COEF * float(all_items * media_total) / total_count
     query_own, keyval_own, output_own = (
-        lax.all_gather(query_weight, "wide", axis=0, tiled=True),
+        ring_gather(query_weight, "wide", 0),
         lax.all_gather(keyval_weight, "wide", axis=0, tiled=True),
         lax.all_gather(output_weight, "wide", axis=1, tiled=True),
     )

time: 944 us -> 911 us (0.965)
  waiting for transfers between devices: 649 us -> 586 us
  starting transfers between devices: 9.14 us -> 27.4 us
  local copies, waits for them, and re-layouts: 54.7 us -> 70.3 us
    all_gather x1, waiting for transfers between devices: 51.6 us -> 0.02 us  [body(): lax.all_gather(keyval_weight, 'wide', axis=0, tiled=True)]
    all_gather x1 -> x0, waiting for transfers between devices: 30.5 us -> none  [body(): lax.all_gather(query_weight, 'wide', axis=0, tiled=True)]
    ppermute x0 -> x7, starting transfers between devices: none -> 18.3 us  [the longest x3 12.6 us: ring_gather(): upper.append(lax.ppermute(upper[-1] if upper else x, axis, back))]
    ppermute x0 -> x7, waiting for transfers between devices: none -> 16.9 us  [the longest x4 16.9 us: ring_gather(): lower.append(lax.ppermute(lower[-1] if lower else x, axis, pairs))]
    unnamed x128 -> x137, local copies, waits for them, and re-layouts: 15.5 us -> 27.4 us
    unnamed x17 -> x16, waiting for transfers between devices: 187 us -> 185 us
  transfers between devices with their start and end apart: 17 -> 23, of which waited for: 14 -> 16; matrix products, arithmetic and copies ran while one was open for 16% -> 18% of each run, Pallas kernels for 0% -> 0%
where the time goes in v1:
time: 911 us; the launch traced here: 908 us
  waiting for transfers between devices  586 us (64%)
  matrix products  93.2 us (10%)
  blocking collectives  86.1 us (9%)
  local copies, waits for them, and re-layouts  70.3 us (8%)
  other arithmetic  28.3 us (3%)
  starting transfers between devices  27.4 us (3%)
  between operations  17.4 us (2%)
    unnamed x16, waiting for transfers between devices  185 us
    reduce_scatter x1, waiting for transfers between devices, body(): lax.psum_scatter(up_acc.astype(jnp.bfloat16), 'wide', scatter_dimension=0...  97 us
    reduce_scatter x1, waiting for transfers between devices, body(): lax.psum_scatter(down_acc.astype(jnp.bfloat16), 'wide', scatter_dimension...  96.6 us
    all_gather x1, waiting for transfers between devices, item_step(): lax.all_gather(media_nf.astype(jnp.bfloat16), 'narrow', axis=0, tiled=True)  43.9 us
    unnamed x1, blocking collectives  40.1 us
    reduce_scatter x1, waiting for transfers between devices, body(): lax.psum_scatter(query_acc.astype(jnp.bfloat16), 'wide', scatter_dimensio...  32.6 us
    all_to_all x1, waiting for transfers between devices, item_step(): lax.all_to_all(media_pairs, 'narrow', split_axis=0, concat_axis=2, tiled=...  31.9 us
    all_gather x1, waiting for transfers between devices, body(): lax.all_gather(query_own, 'narrow', axis=1, tiled=True)  30.3 us
  transfers between devices with their start and end apart: 23, of which 16 were waited for; matrix products, arithmetic and copies ran while one was open for 18% of the time, Pallas kernels for 0%

profile of v1, /device:TPU:0, one launch (start us, length us, event | category | flops | bytes accessed | tf_op | source)
XLA Modules:
  0.0 908.3 jit_solution(5497624061497213550)
XLA Ops:
  28.6 8.2 collective-permute-done.1
  45.0 5.6 all_gather.33
  77.2 43.9 %all-gather.7.cloned.1.call-done = bf16[2048,1536]{1,0:T(8,128)(2,1)} async-done(((bf16[512,1536]{1,0:T(8,128)(2,1)}), bf16[2048,1536]{1,0:T(8,128)(2,1)}) %all-gather.7.cloned.1.call-update) | async-done | bytes 6291472 | tf_op jit(solution)/shard_map/while/body/eval_jaxpr/all_gather | solution.py:137
  124.6 5.5 convolution_convert_fusion.2
  148.0 16.5 %all-gather.11.cloned.1.call-done = bf16[384,1536]{0,1:T(8,128)(2,1)} async-done(((bf16[384,192]{0,1:T(8,128)(2,1)}), bf16[384,1536]{0,1:T(8,128)(2,1)}) %all-gather.11.cloned.1.call-update) | async-done | bytes 1179664 | tf_op jit(solution)/shard_map/all_gather | solution.py:101
  167.0 7.1 all-gather
  174.1 11.8 %reduce-scatter.11.cloned.1.call-done = bf16[16,1536]{1,0:T(8,128)(2,1)} async-done(((bf16[64,1536]{1,0:T(8,128)(2,1)}), bf16[16,1536]{1,0:T(8,128)(2,1)}) %reduce-scatter.11.cloned.1.call-update) | async-done | bytes 49168 | tf_op jit(solution)/shard_map/while/body/eval_jaxpr/reduce_scatter | solution.py:168
  188.7 5.6 all_gather.36
  208.3 19.3 %reduce-scatter.15.cloned.1.call-done = bf16[16,1536]{1,0:T(8,128)(2,1)} async-done(((bf16[64,1536]{1,0:T(8,128)(2,1)}), bf16[16,1536]{1,0:T(8,128)(2,1)}) %reduce-scatter.15.cloned.1.call-update) | async-done | bytes 49168 | tf_op jit(solution)/shard_map/while/body/eval_jaxpr/reduce_scatter | solution.py:195
  230.0 5.8 all_gather.38
  239.7 21.9 %psum.7 = f32[]{:T(128)} all-reduce(f32[]{:T(128)S(6)} %add.222), channel_id=1, replica_groups=mesh['wide'=8,'narrow'=4] {'wide'}, use_global_device_ids=true, to_apply=%region_14.15 | all-reduce | flops 1 | bytes 8 | tf_op jit(solution)/shard_map/psum | solution.py:95
  282.2 10.4 %convolution_convert_fusion.4 = bf16[1536,768]{0,1:T(8,128)(2,1)} fusion(bf16[2112,1536]{1,0:T(8,128)(2,1)} %copy-done.6, bf16[2112,384]{0,1:T(8,128)(2,1)S(1)} %bitcast.181, bf16[2112,384]{0,1:T(8,128)(2,1)S(1)} %bitcast.174), kind=kOutput, calls=%fused_computation.20 | convolution fusion | flops 4990500864 | bytes 12091392 | tf_op jit(solution)/shard_map/while/body/eval_jaxpr/kd,ke->de/dot_general | solution.py:237
  292.6 6.9 copy.135
  303.6 8.8 copy.126
  322.1 31.9 %all-to-all-done = bf16[2048,2,384]{2,1,0:T(2,128)(2,1)} async-done(((bf16[2048,2,384]{2,1,0:T(2,128)(2,1)}), bf16[2048,2,384]{2,1,0:T(2,128)(2,1)}, u32[]{:S(2)}, u32[]{:S(2)}) %all-to-all-start) | async-done | bytes 3145760 | tf_op jit(solution)/shard_map/while/body/eval_jaxpr/all_to_all | solution.py:252
  358.3 10.0 %multiply_reduce_fusion = (f32[1536]{0:T(1024)}, f32[512]{0:T(512)S(1)}, f32[512]{0:T(512)S(1)}, f32[1536]{0:T(1024)}, f32[512,1536]{1,0:T(8,128)S(1)}) fusion(f32[512,1536]{1,0:T(8,128)S(1)} %get-tuple-element.150, f32[512]{0:T(512)S(1)} %add_rsqrt_fusion, f32[512]{0:T(512)S(1)} %broadcast_multiply_fusion.2, f32[1536]{0:T(1024)S(1)} %copy-done.33, ...), kind=kOutput, calls=%fused_computation.24 | convolution fusion | flops 4838912000 | bytes 18900992 | tf_op jit(solution)/shard_map/while/body/eval_jaxpr/rsc,dsc->rd/dot_general | solution.py:255
  396.4 32.6 %reduce-scatter.17.cloned.1.call-done = bf16[192,384]{1,0:T(8,128)(2,1)} async-done(((bf16[1536,384]{1,0:T(8,128)(2,1)}), bf16[192,384]{1,0:T(8,128)(2,1)}) %reduce-scatter.17.cloned.1.call-update) | async-done | bytes 147472 | tf_op jit(solution)/shard_map/reduce_scatter | solution.py:328
  430.7 109.6 %all-reduce.11.cloned.1.call-done = bf16[1536,2,384]{2,1,0:T(2,128)(2,1)} async-done(((bf16[1536,2,384]{2,1,0:T(2,128)(2,1)}), bf16[1536,2,384]{2,1,0:T(2,128)(2,1)}) %all-reduce.11.cloned.1.call-update) | async-done | bytes 2359312
  542.2 6.2 convolution_bitcast_fusion.2
  548.6 30.3 %all-gather.15.cloned.1.call-done = bf16[1536,1536]{1,0:T(8,128)(2,1)} async-done(((bf16[1536,384]{1,0:T(8,128)(2,1)}), bf16[1536,1536]{1,0:T(8,128)(2,1)}) %all-gather.15.cloned.1.call-update) | async-done | bytes 4718608 | tf_op jit(solution)/shard_map/all_gather | solution.py:104
  582.7 40.1 %all-reduce.8 = (f32[1536]{0:T(1024)S(1)}, f32[1536]{0:T(1024)S(1)}, f32[1536]{0:T(1024)S(1)}, f32[1536]{0:T(1024)S(1)}, f32[1536]{0:T(1024)S(1)}, /*index=5*/f32[1536]{0:T(1024)S(1)}) all-reduce(f32[1536]{0:T(1024)S(1)} %copy-done.46, f32[1536]{0:T(1024)S(1)} %copy-done.47, ...), channel_id=7, replica_groups=mesh['wide'=8,'narrow'=4] {'wide','narrow'}, use_global_device_ids=true, to_apply=%region_23.24.clone | all-reduce | flops 9216 | bytes 73728
  627.9 74.4 %reduce-scatter.25.cloned.1.call-done = f32[48,8]{1,0:T(8,128)} async-done(((f32[1536,8]{1,0:T(8,128)}), f32[48,8]{1,0:T(8,128)}) %reduce-scatter.25.cloned.1.call-update) | async-done | bytes 1552
  703.8 97.0 %reduce-scatter.21.cloned.1.call-done = bf16[192,1536]{1,0:T(8,128)(2,1)} async-done(((bf16[1536,1536]{1,0:T(8,128)(2,1)}), bf16[192,1536]{1,0:T(8,128)(2,1)}) %reduce-scatter.21.cloned.1.call-update) | async-done | bytes 589840 | tf_op jit(solution)/shard_map/reduce_scatter | solution.py:322
  803.0 96.6 %reduce-scatter.23.cloned.1.call-done = bf16[1536,192]{0,1:T(8,128)(2,1)} async-done(((bf16[1536,1536]{0,1:T(8,128)(2,1)}), bf16[1536,192]{0,1:T(8,128)(2,1)}) %reduce-scatter.23.cloned.1.call-update) | async-done | bytes 589840 | tf_op jit(solution)/shard_map/reduce_scatter | solution.py:325
  (266 shorter events, 185.1 us)
Async XLA Ops:
  7.2 65.8 %all-gather.9.cloned.1.call-start = ((), (), s32[]{:S(2)}) async-start(), calls=%async_computation.11 | async-start | bytes 2654208 | tf_op jit(solution)/shard_map/all_gather | solution.py:100
  9.0 112.2 %all-gather.7.cloned.1.call-start = ((), (), s32[]{:S(2)}) async-start(), calls=%async_computation.10 | async-start | bytes 7864320 | tf_op jit(solution)/shard_map/while/body/eval_jaxpr/all_gather | solution.py:137
  13.7 150.8 %all-gather.11.cloned.1.call-start = ((), (), s32[]{:S(2)}) async-start(), calls=%async_computation.12 | async-start | bytes 1327104 | tf_op jit(solution)/shard_map/all_gather | solution.py:101
  13.7 11.6 %collective-permute-start = (bf16[192,384]{1,0:T(8,128)(2,1)S(1)}, bf16[192,384]{1,0:T(8,128)(2,1)}, u32[]{:S(2)}, u32[]{:S(2)}) collective-permute-start(bf16[192,384]{1,0:T(8,128)(2,1)S(1)} %copy-done.28), channel_id=1, source_target_pairs={{0,4},{4,8},{8,12},{12,16},{16,20},{20,24},{24,28},{28,0},{1,5},{5... | collective-permute-start | bytes 442376 | tf_op jit(solution)/shard_map/ppermute | solution.py:29
  16.8 20.7 %collective-permute-start.4 = (bf16[192,384]{1,0:T(8,128)(2,1)S(1)}, bf16[192,384]{1,0:T(8,128)(2,1)}, u32[]{:S(2)}, u32[]{:S(2)}) collective-permute-start(bf16[192,384]{1,0:T(8,128)(2,1)S(1)} %copy-done.28), channel_id=1, source_target_pairs={{4,0},{8,4},{12,8},{16,12},{20,16},{24,20},{28,24},{0,28},{5,1},{9... | collective-permute-start | bytes 442376 | tf_op jit(solution)/shard_map/ppermute | solution.py:31
  19.9 166.0 %reduce-scatter.11.cloned.1.call-start = ((), (), s32[]{:S(2)}) async-start(), calls=%async_computation.13 | async-start | bytes 245760 | tf_op jit(solution)/shard_map/while/body/eval_jaxpr/reduce_scatter | solution.py:168
  25.3 11.5 %collective-permute-start.1 = (bf16[192,384]{1,0:T(8,128)(2,1)}, bf16[192,384]{1,0:T(8,128)(2,1)}, u32[]{:S(2)}, u32[]{:S(2)}) collective-permute-start(bf16[192,384]{1,0:T(8,128)(2,1)} %collective-permute-done), channel_id=1, source_target_pairs={{0,4},{4,8},{8,12},{12,16},{16,20},{20,24},{24,28},{28,0},{1,5},{5... | collective-permute-start | bytes 442376 | tf_op jit(solution)/shard_map/ppermute | solution.py:29
  36.8 8.2 collective-permute-start.2
  37.5 13.1 %collective-permute-start.5 = (bf16[192,384]{1,0:T(8,128)(2,1)}, bf16[192,384]{1,0:T(8,128)(2,1)}, u32[]{:S(2)}, u32[]{:S(2)}) collective-permute-start(bf16[192,384]{1,0:T(8,128)(2,1)} %collective-permute-done.4), channel_id=1, source_target_pairs={{4,0},{8,4},{12,8},{16,12},{20,16},{24,20},{28,24},{0,28},{5,1},{9... | collective-permute-start | bytes 442376 | tf_op jit(solution)/shard_map/ppermute | solution.py:31
  45.0 11.4 %collective-permute-start.3 = (bf16[192,384]{1,0:T(8,128)(2,1)}, bf16[192,384]{1,0:T(8,128)(2,1)}, u32[]{:S(2)}, u32[]{:S(2)}) collective-permute-start(bf16[192,384]{1,0:T(8,128)(2,1)} %collective-permute-done.2), channel_id=1, source_target_pairs={{0,4},{4,8},{8,12},{12,16},{16,20},{20,24},{24,28},{28,0},{1,5},{5... | collective-permute-start | bytes 442376 | tf_op jit(solution)/shard_map/ppermute | solution.py:29
  50.7 16.9 %collective-permute-start.6 = (bf16[192,384]{1,0:T(8,128)(2,1)}, bf16[192,384]{1,0:T(8,128)(2,1)S(1)}, u32[]{:S(2)}, u32[]{:S(2)}) collective-permute-start(bf16[192,384]{1,0:T(8,128)(2,1)} %collective-permute-done.5), channel_id=1, source_target_pairs={{4,0},{8,4},{12,8},{16,12},{20,16},{24,20},{28,24},{0,28},{5,1},{9... | collective-permute-start | bytes 442376 | tf_op jit(solution)/shard_map/ppermute | solution.py:31
  167.0 60.6 %reduce-scatter.15.cloned.1.call-start = ((), (), s32[]{:S(2)}) async-start(), calls=%async_computation.15 | async-start | bytes 245760 | tf_op jit(solution)/shard_map/while/body/eval_jaxpr/reduce_scatter | solution.py:195
  207.6 150.6 %all-gather.13.cloned.1.call-start = ((), (), s32[]{:S(2)}) async-start(), calls=%async_computation.16 | async-start | bytes 11796480 | tf_op jit(solution)/shard_map/all_gather | solution.py:105
  208.2 186.5 %reduce-scatter.19.cloned.1.call-start = ((), (), s32[]{:S(2)}) async-start(), calls=%async_computation.19 | async-start | bytes 1327104 | tf_op jit(solution)/shard_map/reduce_scatter | solution.py:337
  239.0 190.1 %reduce-scatter.17.cloned.1.call-start = ((), (), s32[]{:S(2)}) async-start(), calls=%async_computation.18 | async-start | bytes 1327104 | tf_op jit(solution)/shard_map/reduce_scatter | solution.py:328
  278.7 261.5 %all-reduce.11.cloned.1.call-start = ((), (), s32[]{:S(2)}) async-start(), calls=%async_computation.23 | async-start | bytes 4718592
  299.5 279.3 %all-gather.15.cloned.1.call-start = ((), (), s32[]{:S(2)}) async-start(), calls=%async_computation.17 | async-start | bytes 5898240 | tf_op jit(solution)/shard_map/all_gather | solution.py:104
  312.4 41.6 %all-to-all-start = ((bf16[2048,2,384]{2,1,0:T(2,128)(2,1)}), bf16[2048,2,384]{2,1,0:T(2,128)(2,1)}, u32[]{:S(2)}, u32[]{:S(2)}) async-start(bf16[2048,2,384]{2,1,0:T(2,128)(2,1)} %copy.126), calls=%async_computation.3 | async-start | bytes 6291456 | tf_op jit(solution)/shard_map/while/body/eval_jaxpr/all_to_all | solution.py:252
  317.1 309.3 %reduce-scatter.13.cloned.1.call-start = ((), (), s32[]{:S(2)}) async-start(), calls=%async_computation.14 | async-start | bytes 245760 | tf_op jit(solution)/shard_map/while/body/eval_jaxpr/reduce_scatter | solution.py:180
  321.8 380.5 %reduce-scatter.25.cloned.1.call-start = ((), (), s32[]{:S(2)}) async-start(), calls=%async_computation.22 | async-start | bytes 811008
  374.0 426.8 %reduce-scatter.21.cloned.1.call-start = ((), (), s32[]{:S(2)}) async-start(), calls=%async_computation.20 | async-start | bytes 5308416 | tf_op jit(solution)/shard_map/reduce_scatter | solution.py:322
  377.6 521.9 %reduce-scatter.23.cloned.1.call-start = ((), (), s32[]{:S(2)}) async-start(), calls=%async_computation.21 | async-start | bytes 5308416 | tf_op jit(solution)/shard_map/reduce_scatter | solution.py:325
  386.1 8.6 all-to-all-start.1
  578.8 322.9 %copy-start.1 = (bf16[8,1536]{1,0:T(8,128)(2,1)S(1)}, bf16[8,1536]{1,0:T(8,128)(2,1)}, u32[]{:S(2)}) copy-start(bf16[8,1536]{1,0:T(8,128)(2,1)} %param.21) | copy-start | bytes 73732
  (59 other events, 1367.2 us)
Sparse Core Ops, SparseCore 0:
  10.8 61.7 all-gather.8
  74.7 46.3 all-gather.6
  123.3 41.1 all-gather.10
  167.4 18.4 reduce-scatter.10
  207.8 19.7 reduce-scatter.14
  229.0 64.0 all-gather.12
  296.5 64.6 reduce-scatter.18
  365.2 63.7 reduce-scatter.16
  432.6 107.5 all-reduce.10
  542.3 36.5 all-gather.14
  581.3 19.8 reduce-scatter.12
  606.1 96.2 reduce-scatter.24
  706.0 94.7 reduce-scatter.20
  804.3 95.2 reduce-scatter.22
